TPU v7x, 512 devices: a whole 4x8x8 slice. The times are simulated.
512 devices in a mesh: sec: 64 (over x, y, core), mp: 8 (over z).
Axes of the slice: x: 4, y: 8, z: 8, core: 2. Of those that a mesh axis runs over, the one named last changes fastest.
Arguments:
- inputs: bfloat16 [8192, 2048], P('sec'), may hold values from -6 to 6
- expert_w: bfloat16 [8, 2048, 1024], P('mp', 'sec'), may hold values from -0.125 to 0.125
- gate_w: bfloat16 [2048, 6, 8], replicated, may hold values from -0.125 to 0.125
- tower_up: bfloat16 [64, 1024, 4096], P('sec', None, 'mp'), as said below
- tower_out: bfloat16 [64, 4096], P('sec', 'mp'), as said below
- sections: int32 [64], replicated, may hold values from 0 to 5, as said below
- tasks: int32 [8192, 6], P('sec'), may hold values from 0 to 1, as said below
- labels: int32 [8192, 6], P('sec'), may hold values 0 or 1
Outputs:
- input_grad: bfloat16 [8192, 2048], P('sec', 'mp')
Inputs may be any that keep to these rules, and one draw needn't show every extreme that they name: `sections`: each task owns one run of consecutive indices, the runs in task order, every task at least one index. `tasks`: in each aligned block of 128 examples, task t has at most 4 times as many examples as its section has indices of sec; every task reaches this bound in some block. `tower_up`: all indices of one section hold equal copies. `tower_out`: all indices of one section hold equal copies.
All inputs are finite; a program needn't handle non-finite values. No bound on the sum of `labels` on one device may be relied on, other than what follows from the above.
Results may differ from a plain program's by a relative error of at most 0.024.
Values may be sent and summed in bfloat16 or wider, within the bound.
No kernel may reach another device: no remote copies, remote signals or barrier semaphores. Data moves between devices by JAX's collectives and lax.ppermute only.
A program may use at most 64 MiB of HBM per device.

v0:
```python
import jax
import jax.numpy as jnp
from jax import lax
from jax.sharding import PartitionSpec as P

loss_scale = 64.0


def silu_slope(value, sig):
    return sig * (1.0 + value * (1.0 - sig))


def per_device(inputs, expert_w, gate_w, tower_up, tower_out, sections, tasks, labels):
    rows = inputs.shape[0]
    task_count = tasks.shape[1]
    n_sec = lax.axis_size("sec")
    pair_slots = 2 * rows // n_sec
    slots = n_sec * pair_slots
    local_w = expert_w[0]
    width = local_w.shape[1]
    picker = (jnp.arange(gate_w.shape[2], dtype=jnp.int32) == lax.axis_index("mp")).astype(
        jnp.float32
    )
    gate_logit = jnp.einsum("nd,dtk->ntk", inputs, gate_w, preferred_element_type=jnp.float32)
    raised = jnp.exp(gate_logit)
    gates = raised / jnp.sum(raised, axis=2, keepdims=True)
    mine = jnp.sum(gates * picker, axis=2)
    whole_w = lax.all_gather(local_w, "sec", axis=0, tiled=True)
    pre = jnp.dot(inputs, whole_w, preferred_element_type=jnp.float32)
    sig_pre = jax.nn.sigmoid(pre)
    expert_out = (pre * sig_pre).astype(jnp.bfloat16)
    task_ids = jnp.arange(task_count, dtype=jnp.int32)
    members = jnp.sum((sections[None, :] == task_ids[:, None]).astype(jnp.int32), axis=1)
    first = jnp.sum((sections[None, :] < task_ids[:, None]).astype(jnp.int32), axis=1)
    ranks = jnp.cumsum(tasks, axis=0) - tasks
    target = first[None, :] + ranks % members[None, :]
    place = target * pair_slots + ranks // members[None, :]
    place = jnp.where(tasks > 0, place, slots)
    pair_total = rows * task_count
    pair_ids = jnp.arange(pair_total, dtype=jnp.int32)
    source = (
        jnp.full((slots,), pair_total, jnp.int32).at[place.reshape(-1)].set(pair_ids, mode="drop")
    )
    filled = (source < pair_total).astype(jnp.float32)
    source = jnp.minimum(source, pair_total - 1)
    src_row = source // task_count
    src_task = source % task_count
    weight = mine[src_row, src_task] * filled
    contrib = weight[:, None] * expert_out[src_row].astype(jnp.float32)
    tag_out = (filled * (1.0 + labels[src_row, src_task].astype(jnp.float32))).astype(jnp.bfloat16)
    sent = lax.psum(contrib.astype(jnp.bfloat16), "mp")
    arrived, tag_in = (
        lax.all_to_all(
            sent.reshape(n_sec, pair_slots, -1), "sec", split_axis=0, concat_axis=0, tiled=True
        ),
        lax.all_to_all(
            tag_out.reshape(n_sec, pair_slots), "sec", split_axis=0, concat_axis=0, tiled=True
        ),
    )
    arrived = arrived.reshape(slots, -1)
    up_local = tower_up[0]
    out_local = tower_out[0].astype(jnp.float32)
    act = jnp.dot(arrived, up_local, preferred_element_type=jnp.float32)
    sig_act = jax.nn.sigmoid(act)
    partial_logit = jnp.sum(act * sig_act * out_local[None, :], axis=1)
    logit = lax.psum(partial_logit, "mp")
    tag_value = tag_in.reshape(slots).astype(jnp.float32)
    alive = (tag_value > 0.5).astype(jnp.float32)
    label_value = jnp.maximum(tag_value - 1.0, 0.0)
    slope = loss_scale * (jax.nn.sigmoid(logit) - label_value) * alive
    act_grad = (slope[:, None] * out_local[None, :] * silu_slope(act, sig_act)).astype(jnp.bfloat16)
    back = lax.dot_general(
        act_grad, up_local, (((1,), (1,)), ((), ())), preferred_element_type=jnp.float32
    )
    grads = lax.psum(back.astype(jnp.bfloat16), "mp")
    returned = lax.all_to_all(
        grads.reshape(n_sec, pair_slots, -1), "sec", split_axis=0, concat_axis=0, tiled=True
    ).reshape(slots, -1)
    padded = jnp.concatenate([returned, jnp.zeros((1, width), jnp.bfloat16)], axis=0)
    mixture_grad = padded[place]
    expert_grad = jnp.zeros((rows, width), jnp.float32)
    for task in range(task_count):
        expert_grad = expert_grad + mine[:, task : task + 1] * mixture_grad[:, task].astype(
            jnp.float32
        )
    gate_grad = jnp.einsum(
        "nte,ne->nt", mixture_grad, expert_out, preferred_element_type=jnp.float32
    )
    spread_sum = lax.psum(mine * gate_grad, "mp")
    gate_logit_grad = mine * (gate_grad - spread_sum)
    pre_grad = (expert_grad * silu_slope(pre, sig_pre)).astype(jnp.bfloat16)
    gate_cols = jnp.sum(gate_w.astype(jnp.float32) * picker, axis=2)
    gate_part = jnp.dot(gate_logit_grad, gate_cols.T, precision=lax.Precision.HIGHEST)
    input_part = lax.dot_general(
        pre_grad, whole_w, (((1,), (1,)), ((), ())), preferred_element_type=jnp.float32
    )
    return lax.psum_scatter(
        (input_part + gate_part).astype(jnp.bfloat16), "mp", scatter_dimension=1, tiled=True
    )


def solution(mesh):
    in_specs = (
        P("sec", None),
        P("mp", "sec", None),
        P(),
        P("sec", None, "mp"),
        P("sec", "mp"),
        P(),
        P("sec", None),
        P("sec", None),
    )
    out_specs = P("sec", "mp")
    return jax.shard_map(
        per_device, mesh=mesh, in_specs=in_specs, out_specs=out_specs, check_vma=False
    )
```

profile of v0, /device:TPU:2, one launch (start us, length us, event | category | flops | bytes accessed | tf_op | source)
XLA Modules:
  0.0 409.1 jit_solution(17913889090033370645)
XLA Ops:
  6.5 0.7 all-gather.3.cloned.1.call-update
  7.3 0.8 copy.35
  8.1 0.7 broadcast_compare_fusion
  9.1 0.8 convert_reduce_fusion.1
  9.9 1.3 compare_select_fusion
  11.4 3.4 scatter_custom_fusion
  14.8 1.4 fusion.54
  16.3 1.4 gather_fusion.1
  17.6 1.4 gather_fusion
  19.1 79.5 %all-gather.3.cloned.1.call-done = bf16[1,2048,1024]{2,1,0:T(8,128)(2,1)} async-done(((bf16[1,32,1024]{2,1,0:T(8,128)(2,1)}), bf16[1,2048,1024]{2,1,0:T(8,128)(2,1)}) %all-gather.3.cloned.1.call-update) | async-done | bytes 4194320 | tf_op jit(solution)/shard_map/all_gather | solution.py:28
  98.6 3.8 multiply_convert_fusion.2
  102.4 1.2 gather_fusion.2
  103.7 1.0 reshape.94
  104.9 16.0 %all_to_all.20 = bf16[64,1,4]{2,1,0:T(2,128)(2,1)S(1)} all-to-all(bf16[64,1,4]{2,1,0:T(2,128)(2,1)S(1)} %all_to_all.16), channel_id=1, replica_groups=mesh['sec'=64,'mp'=8] {'sec'}, dimensions={0} | all-to-all | bytes 1024 | tf_op jit(solution)/shard_map/all_to_all | solution.py:56
  120.8 62.6 %all-reduce.4.cloned.1.call-done = bf16[64,4,1024]{2,1,0:T(4,128)(2,1)} async-done(((bf16[64,4,1024]{2,1,0:T(4,128)(2,1)}), bf16[64,4,1024]{2,1,0:T(4,128)(2,1)}) %all-reduce.4.cloned.1.call-update) | async-done | bytes 524304 | tf_op jit(solution)/shard_map/psum | solution.py:51
  183.4 10.3 %all-to-all-start.1 = ((bf16[64,4,1024]{2,1,0:T(4,128)(2,1)}), bf16[64,4,1024]{2,1,0:T(4,128)(2,1)S(1)}, u32[]{:S(2)}, u32[]{:S(2)}) async-start(bf16[64,4,1024]{2,1,0:T(4,128)(2,1)} %all-reduce.4.cloned.1.call-done), calls=%async_computation.1 | async-start | bytes 1048576 | tf_op jit(solution)/shard_map/all_to_all | solution.py:53
  194.3 16.1 %all-to-all-done.1 = bf16[64,4,1024]{2,1,0:T(4,128)(2,1)S(1)} async-done(((bf16[64,4,1024]{2,1,0:T(4,128)(2,1)}), bf16[64,4,1024]{2,1,0:T(4,128)(2,1)S(1)}, u32[]{:S(2)}, u32[]{:S(2)}) %all-to-all-start.1) | async-done | bytes 524320 | tf_op jit(solution)/shard_map/all_to_all | solution.py:53
  210.5 0.6 multiply_reduce_fusion
  211.1 16.3 %psum.29 = f32[256]{0:T(256)S(1)} all-reduce(f32[256]{0:T(256)S(1)} %get-tuple-element.29), channel_id=1, replica_groups=mesh['sec'=64,'mp'=8] {'mp'}, use_global_device_ids=true, to_apply=%region_8.9 | all-reduce | flops 256 | bytes 2048 | tf_op jit(solution)/shard_map/psum | solution.py:66
  227.4 0.7 convolution_convert_fusion
  228.1 1.0 reshape.96
  229.1 75.2 %all-reduce.6.cloned.1.call-done = bf16[64,4,1024]{2,1,0:T(4,128)(2,1)} async-done(((bf16[64,4,1024]{2,1,0:T(4,128)(2,1)}), bf16[64,4,1024]{2,1,0:T(4,128)(2,1)}) %all-reduce.6.cloned.1.call-update) | async-done | bytes 524304 | tf_op jit(solution)/shard_map/psum | solution.py:75
  304.4 10.3 %all-to-all-start.2 = ((bf16[64,4,1024]{2,1,0:T(4,128)(2,1)}), bf16[64,4,1024]{2,1,0:T(4,128)(2,1)S(1)}, u32[]{:S(2)}, u32[]{:S(2)}) async-start(bf16[64,4,1024]{2,1,0:T(4,128)(2,1)} %all-reduce.6.cloned.1.call-done), calls=%async_computation.2 | async-start | bytes 1048576 | tf_op jit(solution)/shard_map/all_to_all | solution.py:76
  315.8 15.5 %all-to-all-done.2 = bf16[64,4,1024]{2,1,0:T(4,128)(2,1)S(1)} async-done(((bf16[64,4,1024]{2,1,0:T(4,128)(2,1)}), bf16[64,4,1024]{2,1,0:T(4,128)(2,1)S(1)}, u32[]{:S(2)}, u32[]{:S(2)}) %all-to-all-start.2) | async-done | bytes 524320 | tf_op jit(solution)/shard_map/all_to_all | solution.py:76
  331.5 3.6 gather_fusion.3
  335.0 2.5 reshape.126
  337.5 3.7 fusion.53
  341.3 1.3 fusion.24
  342.7 16.3 %psum.31 = f32[128,6]{0,1:T(8,128)S(1)} all-reduce(f32[128,6]{0,1:T(8,128)S(1)} %bitcast_multiply_fusion), channel_id=1, replica_groups=mesh['sec'=64,'mp'=8] {'mp'}, use_global_device_ids=true, to_apply=%region_10.11 | all-reduce | flops 768 | bytes 6144 | tf_op jit(solution)/shard_map/psum | solution.py:89
  358.9 1.0 fusion.45
  360.0 6.1 %fusion.8 = bf16[128,2048]{1,0:T(8,128)(2,1)} fusion(f32[128,2048]{1,0:T(8,128)S(1)} %fusion.45, bf16[1,2048,1024]{2,1,0:T(8,128)(2,1)} %all-gather.3.cloned.1.call-done, f32[128,1024]{1,0:T(8,128)} %get-tuple-element.28, bf16[128,1,1024]{2,1,0:T(2,128)(2,1)} %get-tuple-element.16, bf16[128,1,1024]{2,1,0:T(2,128)(2,1)} %get-tuple-element.12, ...), kind=kOutput, calls=%fused_computation.11 | convolution fusion | flops 540803072 | bytes 7867392 | tf_op jit(solution)/shard_map/dot_general | solution.py:94
  366.1 36.4 %reduce-scatter.2.cloned.1.call-done = bf16[128,256]{1,0:T(8,128)(2,1)} async-done(((bf16[128,2048]{1,0:T(8,128)(2,1)}), bf16[128,256]{1,0:T(8,128)(2,1)}) %reduce-scatter.2.cloned.1.call-update) | async-done | bytes 65552 | tf_op jit(solution)/shard_map/reduce_scatter | solution.py:97
  (45 shorter events, 2.8 us)
Async XLA Ops:
  6.5 204.0 %copy-start = (bf16[1,1024,512]{2,1,0:T(8,128)(2,1)S(1)}, bf16[1,1024,512]{2,1,0:T(8,128)(2,1)}, u32[]{:S(2)}) copy-start(bf16[1,1024,512]{2,1,0:T(8,128)(2,1)} %param.11) | copy-start | bytes 3145732
  6.5 92.1 %copy-start.4 = (bf16[128,2048]{1,0:T(8,128)(2,1)S(1)}, bf16[128,2048]{1,0:T(8,128)(2,1)}, u32[]{:S(2)}) copy-start(bf16[128,2048]{1,0:T(8,128)(2,1)} %param.8) | copy-start | bytes 1572868
  6.5 11.1 %copy-start.1 = (s32[128,6]{0,1:T(8,128)S(1)}, s32[128,6]{0,1:T(8,128)}, u32[]{:S(2)}) copy-start(s32[128,6]{0,1:T(8,128)} %param.15) | copy-start | bytes 9220
  6.5 92.0 %all-gather.3.cloned.1.call-start = ((), (), s32[]{:S(2)}) async-start(), calls=%async_computation.7 | async-start | bytes 4259840 | tf_op jit(solution)/shard_map/all_gather | solution.py:28
  7.3 176.2 %all-reduce.4.cloned.1.call-start = ((), (), s32[]{:S(2)}) async-start(), calls=%async_computation.4 | async-start | bytes 1048576 | tf_op jit(solution)/shard_map/psum | solution.py:51
  103.5 90.3 %copy-start.3 = (bf16[1,512]{1,0:T(2,128)(2,1)S(1)}, bf16[1,512]{1,0:T(2,128)(2,1)}, u32[]{:S(2)}) copy-start(bf16[1,512]{1,0:T(2,128)(2,1)} %param.12) | copy-start | bytes 3076
  183.4 26.9 %all-to-all-start.1 = ((bf16[64,4,1024]{2,1,0:T(4,128)(2,1)}), bf16[64,4,1024]{2,1,0:T(4,128)(2,1)S(1)}, u32[]{:S(2)}, u32[]{:S(2)}) async-start(bf16[64,4,1024]{2,1,0:T(4,128)(2,1)} %all-reduce.4.cloned.1.call-done), calls=%async_computation.1 | async-start | bytes 1048576 | tf_op jit(solution)/shard_map/all_to_all | solution.py:53
  193.7 110.6 %all-reduce.6.cloned.1.call-start = ((), (), s32[]{:S(2)}) async-start(), calls=%async_computation.5 | async-start | bytes 1048576 | tf_op jit(solution)/shard_map/psum | solution.py:75
  228.1 87.0 %copy-start.2 = (bf16[2048,6,8]{0,2,1:T(8,128)(2,1)S(1)}, bf16[2048,6,8]{0,2,1:T(8,128)(2,1)}, u32[]{:S(2)}) copy-start(bf16[2048,6,8]{0,2,1:T(8,128)(2,1)} %param.10) | copy-start | bytes 589828
  304.4 26.9 %all-to-all-start.2 = ((bf16[64,4,1024]{2,1,0:T(4,128)(2,1)}), bf16[64,4,1024]{2,1,0:T(4,128)(2,1)S(1)}, u32[]{:S(2)}, u32[]{:S(2)}) async-start(bf16[64,4,1024]{2,1,0:T(4,128)(2,1)} %all-reduce.6.cloned.1.call-done), calls=%async_computation.2 | async-start | bytes 1048576 | tf_op jit(solution)/shard_map/all_to_all | solution.py:76
  314.6 87.9 %reduce-scatter.2.cloned.1.call-start = ((), (), s32[]{:S(2)}) async-start(), calls=%async_computation.6 | async-start | bytes 589824 | tf_op jit(solution)/shard_map/reduce_scatter | solution.py:97
Sparse Core Ops, SparseCore 0:
  10.7 87.8 all-gather.2
  104.9 78.5 all-reduce.3
  229.2 75.0 all-reduce.5
  366.2 36.2 reduce-scatter.1
where the time goes:
time: 410 us; the launch traced here: 409 us
  waiting for transfers between devices  286 us (70%)
  blocking collectives  48.5 us (12%)
  local copies, waits for them, and re-layouts  21.5 us (5%)
  starting transfers between devices  20.9 us (5%)
  matrix products  14.9 us (4%)
  between operations  13.4 us (3%)
    all_gather x1, waiting for transfers between devices, per_device(): whole_w = lax.all_gather(local_w, 'sec', axis=0, tiled=True)  79.5 us
    psum x1, waiting for transfers between devices, per_device(): grads = lax.psum(back.astype(jnp.bfloat16), 'mp')  75.2 us
    psum x1, waiting for transfers between devices, per_device(): sent = lax.psum(contrib.astype(jnp.bfloat16), 'mp')  62.6 us
    reduce_scatter x1, waiting for transfers between devices, per_device(): lax.psum_scatter((input_part + gate_part).astype(jnp.bfloat16), 'mp', sca...  36.4 us
    psum x1, blocking collectives, per_device(): logit = lax.psum(partial_logit, 'mp')  16.3 us
    psum x1, blocking collectives, per_device(): spread_sum = lax.psum(mine * gate_grad, 'mp')  16.3 us
    all_to_all x1, waiting for transfers between devices, per_device(): lax.all_to_all(sent.reshape(n_sec, pair_slots, -1), 'sec', split_axis=0,...  16.1 us
    all_to_all x1, blocking collectives, per_device(): lax.all_to_all(tag_out.reshape(n_sec, pair_slots), 'sec', split_axis=0, c...  16 us
  transfers between devices with their start and end apart: 6, of which 6 were waited for; matrix products, arithmetic and copies ran while one was open for 3% of the time, Pallas kernels for 0%

commit v1 on v0

--- a/solution.py
+++ b/solution.py
@@ -72,7 +72,7 @@
     back = lax.dot_general(
         act_grad, up_local, (((1,), (1,)), ((), ())), preferred_element_type=jnp.float32
     )
-    grads = lax.psum(back.astype(jnp.bfloat16), "mp")
+    grads = jnp.sum(lax.all_gather(back.astype(jnp.bfloat16), "mp"), axis=0)
     returned = lax.all_to_all(
         grads.reshape(n_sec, pair_slots, -1), "sec", split_axis=0, concat_axis=0, tiled=True
     ).reshape(slots, -1)

time: 410 us -> 392 us (0.956)
  waiting for transfers between devices: 286 us -> 265 us
    psum x1 -> x0, waiting for transfers between devices: 75.2 us -> none  [per_device(): grads = lax.psum(back.astype(jnp.bfloat16), 'mp')]
    all_gather x0 -> x1, waiting for transfers between devices: none -> 53.4 us  [per_device(): grads = jnp.sum(lax.all_gather(back.astype(jnp.bfloat16), 'mp'), axis=0)]
where the time goes in v1:
time: 392 us; the launch traced here: 391 us
  waiting for transfers between devices  265 us (68%)
  blocking collectives  47.7 us (12%)
  local copies, waits for them, and re-layouts  21.5 us (5%)
  starting transfers between devices  20.8 us (5%)
  matrix products  15.8 us (4%)
  between operations  13.4 us (3%)
  other arithmetic  6.75 us (2%)
    all_gather x1, waiting for transfers between devices, per_device(): whole_w = lax.all_gather(local_w, 'sec', axis=0, tiled=True)  79.5 us
    psum x1, waiting for transfers between devices, per_device(): sent = lax.psum(contrib.astype(jnp.bfloat16), 'mp')  62.6 us
    all_gather x1, waiting for transfers between devices, per_device(): grads = jnp.sum(lax.all_gather(back.astype(jnp.bfloat16), 'mp'), axis=0)  53.4 us
    reduce_scatter x1, waiting for transfers between devices, per_device(): lax.psum_scatter((input_part + gate_part).astype(jnp.bfloat16), 'mp', sca...  37.3 us
    psum x1, blocking collectives, per_device(): logit = lax.psum(partial_logit, 'mp')  16.2 us
    all_to_all x1, waiting for transfers between devices, per_device(): lax.all_to_all(sent.reshape(n_sec, pair_slots, -1), 'sec', split_axis=0,...  16.1 us
    all_to_all x1, blocking collectives, per_device(): lax.all_to_all(tag_out.reshape(n_sec, pair_slots), 'sec', split_axis=0, c...  16 us
    all_to_all x1, waiting for transfers between devices, per_device(): lax.all_to_all(grads.reshape(n_sec, pair_slots, -1), 'sec', split_axis=0,...  15.5 us
  transfers between devices with their start and end apart: 6, of which 6 were waited for; matrix products, arithmetic and copies ran while one was open for 3% of the time, Pallas kernels for 0%

profile of v1, /device:TPU:2, one launch (start us, length us, event | category | flops | bytes accessed | tf_op | source)
XLA Modules:
  0.0 391.1 jit_solution(6233275253377874821)
XLA Ops:
  6.5 0.7 all-gather.5.cloned.1.call-update
  7.3 0.8 copy.35
  8.1 0.7 broadcast_compare_fusion
  9.1 0.8 convert_reduce_fusion.1
  9.9 1.3 compare_select_fusion
  11.4 3.4 scatter_custom_fusion
  14.8 1.4 fusion.54
  16.3 1.4 gather_fusion.1
  17.6 1.4 gather_fusion
  19.1 79.5 %all-gather.5.cloned.1.call-done = bf16[1,2048,1024]{2,1,0:T(8,128)(2,1)} async-done(((bf16[1,32,1024]{2,1,0:T(8,128)(2,1)}), bf16[1,2048,1024]{2,1,0:T(8,128)(2,1)}) %all-gather.5.cloned.1.call-update) | async-done | bytes 4194320 | tf_op jit(solution)/shard_map/all_gather | solution.py:28
  98.6 3.8 multiply_convert_fusion.2
  102.4 1.2 gather_fusion.2
  103.7 1.0 reshape.94
  104.9 16.0 %all_to_all.20 = bf16[64,1,4]{2,1,0:T(2,128)(2,1)S(1)} all-to-all(bf16[64,1,4]{2,1,0:T(2,128)(2,1)S(1)} %all_to_all.16), channel_id=1, replica_groups=mesh['sec'=64,'mp'=8] {'sec'}, dimensions={0} | all-to-all | bytes 1024 | tf_op jit(solution)/shard_map/all_to_all | solution.py:56
  120.9 62.6 %all-reduce.3.cloned.1.call-done = bf16[64,4,1024]{2,1,0:T(4,128)(2,1)} async-done(((bf16[64,4,1024]{2,1,0:T(4,128)(2,1)}), bf16[64,4,1024]{2,1,0:T(4,128)(2,1)}) %all-reduce.3.cloned.1.call-update) | async-done | bytes 524304 | tf_op jit(solution)/shard_map/psum | solution.py:51
  183.5 10.3 %all-to-all-start.1 = ((bf16[64,4,1024]{2,1,0:T(4,128)(2,1)}), bf16[64,4,1024]{2,1,0:T(4,128)(2,1)S(1)}, u32[]{:S(2)}, u32[]{:S(2)}) async-start(bf16[64,4,1024]{2,1,0:T(4,128)(2,1)} %all-reduce.3.cloned.1.call-done), calls=%async_computation.1 | async-start | bytes 1048576 | tf_op jit(solution)/shard_map/all_to_all | solution.py:53
  194.3 16.1 %all-to-all-done.1 = bf16[64,4,1024]{2,1,0:T(4,128)(2,1)S(1)} async-done(((bf16[64,4,1024]{2,1,0:T(4,128)(2,1)}), bf16[64,4,1024]{2,1,0:T(4,128)(2,1)S(1)}, u32[]{:S(2)}, u32[]{:S(2)}) %all-to-all-start.1) | async-done | bytes 524320 | tf_op jit(solution)/shard_map/all_to_all | solution.py:53
  211.2 16.2 %psum.22 = f32[256]{0:T(256)S(1)} all-reduce(f32[256]{0:T(256)S(1)} %get-tuple-element.29), channel_id=1, replica_groups=mesh['sec'=64,'mp'=8] {'mp'}, use_global_device_ids=true, to_apply=%region_8.9 | all-reduce | flops 256 | bytes 2048 | tf_op jit(solution)/shard_map/psum | solution.py:66
  227.4 1.5 convolution_convert_fusion
  228.9 53.4 %all-gather.7.cloned.1.call-done = bf16[2048,1024]{1,0:T(8,128)(2,1)} async-done(((bf16[256,1024]{1,0:T(8,128)(2,1)}), bf16[2048,1024]{1,0:T(8,128)(2,1)}) %all-gather.7.cloned.1.call-update) | async-done | bytes 4194320 | tf_op jit(solution)/shard_map/all_gather | solution.py:75
  282.3 3.1 reduce_sum.71
  285.4 1.0 reshape.96
  286.4 10.3 %all-to-all-start.2 = ((bf16[64,4,1024]{2,1,0:T(4,128)(2,1)}), bf16[64,4,1024]{2,1,0:T(4,128)(2,1)S(1)}, u32[]{:S(2)}, u32[]{:S(2)}) async-start(bf16[64,4,1024]{2,1,0:T(4,128)(2,1)} %reshape.96), calls=%async_computation.2 | async-start | bytes 1048576 | tf_op jit(solution)/shard_map/all_to_all | solution.py:76
  297.9 15.5 %all-to-all-done.2 = bf16[64,4,1024]{2,1,0:T(4,128)(2,1)S(1)} async-done(((bf16[64,4,1024]{2,1,0:T(4,128)(2,1)}), bf16[64,4,1024]{2,1,0:T(4,128)(2,1)S(1)}, u32[]{:S(2)}, u32[]{:S(2)}) %all-to-all-start.2) | async-done | bytes 524320 | tf_op jit(solution)/shard_map/all_to_all | solution.py:76
  313.5 3.6 gather_fusion.3
  317.1 2.5 reshape.126
  319.6 3.7 fusion.53
  323.3 1.3 fusion.24
  324.7 15.4 %psum.23 = f32[128,6]{0,1:T(8,128)S(1)} all-reduce(f32[128,6]{0,1:T(8,128)S(1)} %bitcast_multiply_fusion), channel_id=1, replica_groups=mesh['sec'=64,'mp'=8] {'mp'}, use_global_device_ids=true, to_apply=%region_10.11 | all-reduce | flops 768 | bytes 6144 | tf_op jit(solution)/shard_map/psum | solution.py:89
  340.2 1.0 fusion.45
  341.2 6.1 %fusion.8 = bf16[128,2048]{1,0:T(8,128)(2,1)} fusion(f32[128,2048]{1,0:T(8,128)S(1)} %fusion.45, bf16[1,2048,1024]{2,1,0:T(8,128)(2,1)} %all-gather.5.cloned.1.call-done, f32[128,1024]{1,0:T(8,128)} %get-tuple-element.28, bf16[128,1,1024]{2,1,0:T(2,128)(2,1)} %get-tuple-element.16, bf16[128,1,1024]{2,1,0:T(2,128)(2,1)} %get-tuple-element.12, ...), kind=kOutput, calls=%fused_computation.11 | convolution fusion | flops 540803072 | bytes 7867392 | tf_op jit(solution)/shard_map/dot_general | solution.py:94
  347.3 37.3 %reduce-scatter.2.cloned.1.call-done = bf16[128,256]{1,0:T(8,128)(2,1)} async-done(((bf16[128,2048]{1,0:T(8,128)(2,1)}), bf16[128,256]{1,0:T(8,128)(2,1)}) %reduce-scatter.2.cloned.1.call-update) | async-done | bytes 65552 | tf_op jit(solution)/shard_map/reduce_scatter | solution.py:97
  (46 shorter events, 3.5 us)
Async XLA Ops:
  6.5 204.0 %copy-start = (bf16[1,1024,512]{2,1,0:T(8,128)(2,1)S(1)}, bf16[1,1024,512]{2,1,0:T(8,128)(2,1)}, u32[]{:S(2)}) copy-start(bf16[1,1024,512]{2,1,0:T(8,128)(2,1)} %param.11) | copy-start | bytes 3145732
  6.5 92.1 %copy-start.4 = (bf16[128,2048]{1,0:T(8,128)(2,1)S(1)}, bf16[128,2048]{1,0:T(8,128)(2,1)}, u32[]{:S(2)}) copy-start(bf16[128,2048]{1,0:T(8,128)(2,1)} %param.8) | copy-start | bytes 1572868
  6.5 11.1 %copy-start.1 = (s32[128,6]{0,1:T(8,128)S(1)}, s32[128,6]{0,1:T(8,128)}, u32[]{:S(2)}) copy-start(s32[128,6]{0,1:T(8,128)} %param.15) | copy-start | bytes 9220
  6.5 92.0 %all-gather.5.cloned.1.call-start = ((), (), s32[]{:S(2)}) async-start(), calls=%async_computation.6 | async-start | bytes 4259840 | tf_op jit(solution)/shard_map/all_gather | solution.py:28
  7.3 176.2 %all-reduce.3.cloned.1.call-start = ((), (), s32[]{:S(2)}) async-start(), calls=%async_computation.4 | async-start | bytes 1048576 | tf_op jit(solution)/shard_map/psum | solution.py:51
  103.6 90.3 %copy-start.3 = (bf16[1,512]{1,0:T(2,128)(2,1)S(1)}, bf16[1,512]{1,0:T(2,128)(2,1)}, u32[]{:S(2)}) copy-start(bf16[1,512]{1,0:T(2,128)(2,1)} %param.12) | copy-start | bytes 3076
  183.5 26.9 %all-to-all-start.1 = ((bf16[64,4,1024]{2,1,0:T(4,128)(2,1)}), bf16[64,4,1024]{2,1,0:T(4,128)(2,1)S(1)}, u32[]{:S(2)}, u32[]{:S(2)}) async-start(bf16[64,4,1024]{2,1,0:T(4,128)(2,1)} %all-reduce.3.cloned.1.call-done), calls=%async_computation.1 | async-start | bytes 1048576 | tf_op jit(solution)/shard_map/all_to_all | solution.py:53
  193.8 88.6 %all-gather.7.cloned.1.call-start = ((), (), s32[]{:S(2)}) async-start(), calls=%async_computation.7 | async-start | bytes 4718592 | tf_op jit(solution)/shard_map/all_gather | solution.py:75
  285.4 11.7 %copy-start.2 = (bf16[2048,6,8]{0,2,1:T(8,128)(2,1)S(1)}, bf16[2048,6,8]{0,2,1:T(8,128)(2,1)}, u32[]{:S(2)}) copy-start(bf16[2048,6,8]{0,2,1:T(8,128)(2,1)} %param.10) | copy-start | bytes 589828
  286.4 26.9 %all-to-all-start.2 = ((bf16[64,4,1024]{2,1,0:T(4,128)(2,1)}), bf16[64,4,1024]{2,1,0:T(4,128)(2,1)S(1)}, u32[]{:S(2)}, u32[]{:S(2)}) async-start(bf16[64,4,1024]{2,1,0:T(4,128)(2,1)} %reshape.96), calls=%async_computation.2 | async-start | bytes 1048576 | tf_op jit(solution)/shard_map/all_to_all | solution.py:76
  296.7 87.9 %reduce-scatter.2.cloned.1.call-start = ((), (), s32[]{:S(2)}) async-start(), calls=%async_computation.5 | async-start | bytes 589824 | tf_op jit(solution)/shard_map/reduce_scatter | solution.py:97
Sparse Core Ops, SparseCore 0:
  10.7 87.8 all-gather.4
  104.9 78.5 all-reduce.2
  229.0 53.2 all-gather.6
  347.4 37.0 reduce-scatter.1
